TPU v7x, 256 devices: a whole 4x4x8 slice. The times are simulated.
256 devices in a mesh: dp: 2 (over y_lo), ulysses: 8 (over x, core), blk: 16 (over y_hi, z).
Axes of the slice: x: 4, y: 4 (y_hi: 2, y_lo: 2; y = y_hi * 2 + y_lo), z: 8, core: 2. Of those that a mesh axis runs over, the one named last changes fastest.
Arguments:
- hidden_in: bfloat16 [2, 16384, 4096], P('dp', ('blk', 'ulysses')), may hold values from -6 to 6
- queries: bfloat16 [2, 16384, 2048], P('dp', ('blk', 'ulysses')), may hold values from -240 to 240
- pair_weight: bfloat16 [4096, 2048], P(('dp', 'blk')), may hold values from -0.09375 to 0.09375
- span_order: int32 [2, 32], P('dp'), may hold values from 0 to 31, each once within a row
- yarn_divisor: int32 [64], replicated, may hold values from 1 to 8
Outputs:
- attended: bfloat16 [2, 16384, 2048], P('dp', ('blk', 'ulysses'))
All inputs are finite; a program needn't handle non-finite values.
Results may differ from a plain program's by a relative error of at most 0.02.
The roundings to bfloat16 on the way count: a program that leaves them out, or rounds other values in their place, can miss the bound.
Values may be sent and summed in bfloat16 or wider, within the bound.
A program may use at most 128 MiB of HBM per device.

v0:
```python
import math

import jax
import jax.numpy as jnp
from jax import lax
from jax.sharding import PartitionSpec as P

KVH = 8
HD = 128
QH = 16
STEPS = 3


LOG_BASE = math.log(500000.0)


def from_behind(block, axis, distance):
    devices = range(lax.axis_size(axis))
    route = [((i - distance) % len(devices), i) for i in devices]
    return lax.ppermute(block, axis, route)


def rotate(vectors, angle_table):
    half_dim = vectors.shape[-1] // 2
    first_half = vectors[..., :half_dim]
    second_half = vectors[..., half_dim:]
    cosine = jnp.cos(angle_table)
    sine_part = jnp.sin(angle_table)
    return jnp.concatenate(
        [
            first_half * cosine - second_half * sine_part,
            second_half * cosine + first_half * sine_part,
        ],
        axis=-1,
    )


def angles(positions, yarn_divisor):
    half_dim = yarn_divisor.shape[0]
    scaled = 2.0 * jnp.arange(half_dim, dtype=jnp.float32) / (2 * half_dim)
    inverse = jnp.exp(-LOG_BASE * scaled) / yarn_divisor.astype(jnp.float32)
    return positions.astype(jnp.float32)[:, None] * inverse[None, :]


def positions_of(order_row, first_row, row_count, span_rows):
    stored = first_row + jnp.arange(row_count, dtype=jnp.int32)
    span_index = stored // span_rows
    matches = span_index[:, None] == jnp.arange(order_row.shape[0], dtype=jnp.int32)[None, :]
    span_value = jnp.sum(jnp.where(matches, order_row[None, :], 0), axis=1)
    return span_value * span_rows + stored % span_rows


def tile_scores(query_rows, key_rows):
    product = lax.dot_general(
        query_rows, key_rows, (((1,), (1,)), ((), ())), preferred_element_type=jnp.float32
    )
    return product * (1.0 / math.sqrt(HD))


def row_maximum(query_rows, query_pos, key_rows, key_pos):
    score = tile_scores(query_rows, key_rows)
    return jnp.max(jnp.where(key_pos[None, :] <= query_pos[:, None], score, -jnp.inf), axis=1)


def add_tile(denominator, numerator, query_rows, query_pos, key_rows, value_rows, key_pos, row_top):
    score = tile_scores(query_rows, key_rows)
    allowed = key_pos[None, :] <= query_pos[:, None]
    weights = jnp.where(allowed, jnp.exp(score - row_top[:, None]), 0.0)
    denominator = denominator + jnp.sum(weights, axis=1)
    numerator = numerator + jnp.dot(
        weights.astype(jnp.bfloat16), value_rows, preferred_element_type=jnp.float32
    )
    return (denominator, numerator)


def shards(hidden_in, queries, pair_weight, span_order, yarn_divisor):
    inputs_local = hidden_in[0]
    queries_local = queries[0]
    order_row = span_order[0]
    token_rows = inputs_local.shape[0]
    ulysses_size = lax.axis_size("ulysses")
    cycle_size = lax.axis_size("blk")
    ulysses_index = lax.axis_index("ulysses")
    cycle_index = lax.axis_index("blk")
    block_rows = token_rows * ulysses_size
    span_rows = block_rows // 2
    kv_width = KVH * HD
    group_size = QH // KVH
    own_positions = positions_of(
        order_row, cycle_index * block_rows + ulysses_index * token_rows, token_rows, span_rows
    )
    own_angles = angles(own_positions, yarn_divisor)
    block_positions = positions_of(order_row, cycle_index * block_rows, block_rows, span_rows)
    rotated_queries = rotate(
        queries_local.astype(jnp.float32).reshape(token_rows, QH, HD), own_angles[:, None, :]
    )
    rotated_queries = rotated_queries.astype(jnp.bfloat16).reshape(token_rows, QH * HD)
    projected = jnp.dot(
        inputs_local,
        lax.all_gather(pair_weight, ("dp", "blk"), axis=0, tiled=True),
        preferred_element_type=jnp.float32,
    )
    token_keys = rotate(
        projected[:, :kv_width].reshape(token_rows, KVH, HD), own_angles[:, None, :]
    )
    token_keys = token_keys.astype(jnp.bfloat16).reshape(token_rows, kv_width)
    token_values = projected[:, kv_width:].astype(jnp.bfloat16)
    query_block, key_block, value_block = (
        lax.all_to_all(rotated_queries, "ulysses", split_axis=1, concat_axis=0, tiled=True),
        lax.all_to_all(token_keys, "ulysses", split_axis=1, concat_axis=0, tiled=True),
        lax.all_to_all(token_values, "ulysses", split_axis=1, concat_axis=0, tiled=True),
    )
    own_pair = jnp.stack([key_block, value_block])
    carried_blocks = [own_pair]
    current_pair = own_pair
    for step_index in range(STEPS):
        current_pair = from_behind(current_pair, "blk", 1)
        carried_blocks.append(current_pair)
    carried_positions = []
    for step_index in range(STEPS + 1):
        source_block = jnp.remainder(cycle_index - step_index, cycle_size)
        carried_positions.append(
            positions_of(order_row, source_block * block_rows, block_rows, span_rows)
        )
    output_rows = []
    for query_half in range(2):
        row_start = query_half * span_rows
        half_positions = block_positions[row_start : row_start + span_rows]
        query_pos = jnp.tile(half_positions, group_size)
        query_part = query_block[row_start : row_start + span_rows, 0 : group_size * HD]
        query_rows = (
            query_part.reshape(span_rows, group_size, HD)
            .transpose(1, 0, 2)
            .reshape(group_size * span_rows, HD)
        )
        tile_list = []
        for step_index in range(STEPS + 1):
            pair_block = carried_blocks[step_index]
            for key_half in range(2):
                key_start = key_half * span_rows
                key_rows = pair_block[0, key_start : key_start + span_rows, 0:HD]
                value_rows = pair_block[1, key_start : key_start + span_rows, 0:HD]
                key_pos = carried_positions[step_index][key_start : key_start + span_rows]
                tile_list.append((key_rows, value_rows, key_pos))
        row_top = jnp.full((group_size * span_rows,), -jnp.inf, jnp.float32)
        for key_rows, value_rows, key_pos in tile_list:
            tile_top = row_maximum(query_rows, query_pos, key_rows, key_pos)
            row_top = jnp.maximum(row_top, tile_top)
        denominator = jnp.zeros((group_size * span_rows,), jnp.float32)
        numerator = jnp.zeros((group_size * span_rows, HD), jnp.float32)
        for key_rows, value_rows, key_pos in tile_list:
            denominator, numerator = add_tile(
                denominator,
                numerator,
                query_rows,
                query_pos,
                key_rows,
                value_rows,
                key_pos,
                row_top,
            )
        normalized = (numerator / denominator[:, None]).astype(jnp.bfloat16)
        normalized = (
            normalized.reshape(group_size, span_rows, HD)
            .transpose(1, 0, 2)
            .reshape(span_rows, group_size * HD)
        )
        output_rows.append(normalized)
    block_output = jnp.concatenate(output_rows, axis=0)
    token_output = lax.all_to_all(block_output, "ulysses", split_axis=0, concat_axis=1, tiled=True)
    return token_output[None]


def solution(mesh):
    return jax.shard_map(
        shards,
        mesh=mesh,
        in_specs=(
            P("dp", ("blk", "ulysses"), None),
            P("dp", ("blk", "ulysses"), None),
            P(("dp", "blk"), None),
            P("dp", None),
            P(),
        ),
        out_specs=P("dp", ("blk", "ulysses"), None),
        check_vma=False,
    )
```

profile of v0, /device:TPU:1, one launch (start us, length us, event | category | flops | bytes accessed | tf_op | source)
XLA Modules:
  0.0 342.1 jit_solution(7863774611345590729)
XLA Ops:
  6.5 0.7 all-gather.2.cloned.1.call-update
  7.3 1.2 copy.29
  9.0 0.8 pad_maximum_fusion
  9.9 6.6 %all-to-all-start = ((bf16[128,8,256]{0,2,1:T(8,128)(2,1)}), bf16[128,8,256]{0,2,1:T(8,128)(2,1)S(1)}, u32[]{:S(2)}, u32[]{:S(2)}) async-start(bf16[128,8,256]{0,2,1:T(8,128)(2,1)} %bitcast.2), calls=%async_computation | async-start | bytes 1048576 | tf_op jit(solution)/shard_map/all_to_all | solution.py:109
  17.1 188.4 %all-gather.2.cloned.1.call-done = bf16[4096,2048]{1,0:T(8,128)(2,1)} async-done(((bf16[128,2048]{1,0:T(8,128)(2,1)}), bf16[4096,2048]{1,0:T(8,128)(2,1)}) %all-gather.2.cloned.1.call-update) | async-done | bytes 16777232 | tf_op jit(solution)/shard_map/all_gather | solution.py:100
  205.5 8.1 %fusion.58 = f32[128,2048]{1,0:T(8,128)S(1)} fusion(bf16[4096,2048]{1,0:T(8,128)(2,1)} %all-gather.2.cloned.1.call-done, bf16[1,128,4096]{2,1,0:T(8,128)(2,1)S(1)} %copy-done), kind=kOutput, calls=%fused_computation.98 | convolution fusion | flops 2147483648 | bytes 18874368 | tf_op jit(solution)/shard_map/dot_general | solution.py:98
  214.2 0.8 pad_maximum_fusion.3
  215.0 5.1 %all-to-all-start.1 = ((bf16[128,8,128]{2,0,1:T(8,128)(2,1)}), bf16[128,8,128]{2,0,1:T(8,128)(2,1)S(1)}, u32[]{:S(2)}, u32[]{:S(2)}) async-start(bf16[128,8,128]{2,0,1:T(8,128)(2,1)} %pad_maximum_fusion.3), calls=%async_computation.1 | async-start | bytes 524288 | tf_op jit(solution)/shard_map/all_to_all | solution.py:110
  220.1 0.7 copy_bitcast_fusion
  220.9 5.7 %all-to-all-done.1 = bf16[128,8,128]{2,0,1:T(8,128)(2,1)S(1)} async-done(((bf16[128,8,128]{2,0,1:T(8,128)(2,1)}), bf16[128,8,128]{2,0,1:T(8,128)(2,1)S(1)}, u32[]{:S(2)}, u32[]{:S(2)}) %all-to-all-start.1) | async-done | bytes 262176 | tf_op jit(solution)/shard_map/all_to_all | solution.py:110
  226.6 4.4 %all-to-all-start.2 = ((bf16[128,8,128]{2,0,1:T(8,128)(2,1)}), bf16[128,8,128]{2,0,1:T(8,128)(2,1)S(1)}, u32[]{:S(2)}, u32[]{:S(2)}) async-start(bf16[128,8,128]{2,0,1:T(8,128)(2,1)} %copy_bitcast_fusion), calls=%async_computation.2 | async-start | bytes 524288 | tf_op jit(solution)/shard_map/all_to_all | solution.py:111
  231.5 5.9 %all-to-all-done.2 = bf16[128,8,128]{2,0,1:T(8,128)(2,1)S(1)} async-done(((bf16[128,8,128]{2,0,1:T(8,128)(2,1)}), bf16[128,8,128]{2,0,1:T(8,128)(2,1)S(1)}, u32[]{:S(2)}, u32[]{:S(2)}) %all-to-all-start.2) | async-done | bytes 262176 | tf_op jit(solution)/shard_map/all_to_all | solution.py:111
  238.0 1.8 fusion.125
  239.8 13.8 %collective-permute-done = bf16[2,1024,128]{2,1,0:T(8,128)(2,1)S(1)} collective-permute-done((bf16[2,1024,128]{2,1,0:T(8,128)(2,1)S(1)}, bf16[2,1024,128]{2,1,0:T(8,128)(2,1)S(1)}, u32[]{:S(2)}, u32[]{:S(2)}) %collective-permute-start) | collective-permute-done | bytes 524320 | tf_op jit(solution)/shard_map/ppermute | solution.py:20
  254.5 1.7 fusion.131
  256.7 12.2 %collective-permute-done.1 = bf16[2,1024,128]{2,1,0:T(8,128)(2,1)S(1)} collective-permute-done((bf16[2,1024,128]{2,1,0:T(8,128)(2,1)S(1)}, bf16[2,1024,128]{2,1,0:T(8,128)(2,1)S(1)}, u32[]{:S(2)}, u32[]{:S(2)}) %collective-permute-start.1) | collective-permute-done | bytes 524320 | tf_op jit(solution)/shard_map/ppermute | solution.py:20
  269.7 1.8 fusion.133
  271.5 1.8 fusion.135
  273.3 9.9 %collective-permute-done.2 = bf16[2,1024,128]{2,1,0:T(8,128)(2,1)S(1)} collective-permute-done((bf16[2,1024,128]{2,1,0:T(8,128)(2,1)S(1)}, bf16[2,1024,128]{2,1,0:T(8,128)(2,1)S(1)}, u32[]{:S(2)}, u32[]{:S(2)}) %collective-permute-start.2) | collective-permute-done | bytes 524320 | tf_op jit(solution)/shard_map/ppermute | solution.py:20
  284.1 2.8 fusion.1
  287.5 4.6 %fusion.18 = (f32[1024]{0:T(1024)S(1)}, f32[1024]{0:T(1024)S(1)}, f32[1024]{0:T(1024)S(1)}, f32[1024]{0:T(1024)S(1)}, f32[1024]{0:T(1024)S(1)}, /*index=5*/f32[1024]{0:T(1024)S(1)}, f32[1024]{0:T(1024)S(1)}, f32[1024]{0:T(1024)S(1)}) fusion(f32[1024,512]{0,1:T(8,128)S(1)} %get-tuple-element.63, f32[1024]{0:T(1024)S(1)} %maximum_maximum_fusion.1, ...), kind=kLoop, calls=%fused_computation.50 | loop fusion | flops 20963328 | bytes 16834560 | tf_op jit(solution)/shard_map/reduce_sum | solution.py:69
  294.9 0.7 fusion.48
  296.4 0.7 fusion.57
  297.1 0.9 copy.37
  298.0 1.5 fusion.137
  299.4 1.3 fusion.139
  300.8 5.0 %fusion.9 = (f32[1024]{0:T(1024)S(1)}, f32[1024]{0:T(1024)S(1)}, f32[1024]{0:T(1024)S(1)}, f32[1024]{0:T(1024)S(1)}, f32[1024]{0:T(1024)S(1)}, /*index=5*/f32[10...) fusion(s32[1024]{0:T(1024)S(1)} %bitcast.165, s32[512]{0:T(512)S(1)} %get-tuple-element.53, ...), kind=kOutput, calls=%fused_computation.41 | convolution fusion | flops 150986752 | bytes 17223680 | tf_op jit(solution)/shard_map/dot_general | solution.py:54
  306.5 0.9 copy-done.5
  307.4 4.8 %fusion.34 = (f32[1024]{0:T(1024)S(1)}, f32[1024]{0:T(1024)S(1)}, f32[1024]{0:T(1024)S(1)}, f32[1024]{0:T(1024)S(1)}, f32[1024]{0:T(1024)S(1)}, /*index=5*/f32[1024]{0:T(1024)S(1)}, f32[1024]{0:T(1024)S(1)}, f32[1024]{0:T(1024)S(1)}) fusion(f32[1024,512]{0,1:T(8,128)S(1)} %get-tuple-element.62, f32[1024]{0:T(1024)S(1)} %maximum_maximum_fusion, ...), kind=kLoop, calls=%fused_computation.66 | loop fusion | flops 20963328 | bytes 16834560 | tf_op jit(solution)/shard_map/reduce_sum | solution.py:69
  317.1 0.7 fusion.56
  318.3 15.7 %all_to_all.58 = bf16[8,128,256]{2,1,0:T(8,128)(2,1)S(1)} all-to-all(bf16[8,128,256]{2,1,0:T(8,128)(2,1)S(1)} %bitcast.151), channel_id=1, replica_groups=mesh['dp'=2,'ulysses'=8,'blk'=16] {'ulysses'}, dimensions={0} | all-to-all | bytes 1048576 | tf_op jit(solution)/shard_map/all_to_all | solution.py:170
  334.3 1.0 copy.43
  (101 shorter events, 16.1 us)
Async XLA Ops:
  6.5 199.0 %copy-start = (bf16[1,128,4096]{2,1,0:T(8,128)(2,1)S(1)}, bf16[1,128,4096]{2,1,0:T(8,128)(2,1)}, u32[]{:S(2)}) copy-start(bf16[1,128,4096]{2,1,0:T(8,128)(2,1)} %param.5) | copy-start | bytes 3145732
  6.5 2.0 copy-start.13
  6.5 2.1 copy-start.14
  6.5 199.0 %all-gather.2.cloned.1.call-start = ((), (), s32[]{:S(2)}) async-start(), calls=%async_computation.4 | async-start | bytes 17301504 | tf_op jit(solution)/shard_map/all_gather | solution.py:100
  9.9 205.2 %all-to-all-start = ((bf16[128,8,256]{0,2,1:T(8,128)(2,1)}), bf16[128,8,256]{0,2,1:T(8,128)(2,1)S(1)}, u32[]{:S(2)}, u32[]{:S(2)}) async-start(bf16[128,8,256]{0,2,1:T(8,128)(2,1)} %bitcast.2), calls=%async_computation | async-start | bytes 1048576 | tf_op jit(solution)/shard_map/all_to_all | solution.py:109
  215.0 11.6 %all-to-all-start.1 = ((bf16[128,8,128]{2,0,1:T(8,128)(2,1)}), bf16[128,8,128]{2,0,1:T(8,128)(2,1)S(1)}, u32[]{:S(2)}, u32[]{:S(2)}) async-start(bf16[128,8,128]{2,0,1:T(8,128)(2,1)} %pad_maximum_fusion.3), calls=%async_computation.1 | async-start | bytes 524288 | tf_op jit(solution)/shard_map/all_to_all | solution.py:110
  226.6 10.9 %all-to-all-start.2 = ((bf16[128,8,128]{2,0,1:T(8,128)(2,1)}), bf16[128,8,128]{2,0,1:T(8,128)(2,1)S(1)}, u32[]{:S(2)}, u32[]{:S(2)}) async-start(bf16[128,8,128]{2,0,1:T(8,128)(2,1)} %copy_bitcast_fusion), calls=%async_computation.2 | async-start | bytes 524288 | tf_op jit(solution)/shard_map/all_to_all | solution.py:111
  237.5 16.1 %collective-permute-start = (bf16[2,1024,128]{2,1,0:T(8,128)(2,1)S(1)}, bf16[2,1024,128]{2,1,0:T(8,128)(2,1)S(1)}, u32[]{:S(2)}, u32[]{:S(2)}) collective-permute-start(bf16[2,1024,128]{2,1,0:T(8,128)(2,1)S(1)} %pad_maximum_fusion.1), channel_id=1, source_target_pairs={{15,0},{0,1},{1,2},{2,3},{3,4},{4,5},{5,6},{6,7},{7,8},{8,9},{9,10... | collective-permute-start | bytes 1572872 | tf_op jit(solution)/shard_map/ppermute | solution.py:20
  253.6 41.3 %copy-start.7 = (bf16[2,1024,128]{2,1,0:T(8,128)(2,1)}, bf16[2,1024,128]{2,1,0:T(8,128)(2,1)S(1)}, u32[]{:S(2)}) copy-start(bf16[2,1024,128]{2,1,0:T(8,128)(2,1)S(1)} %collective-permute-done) | copy-start | bytes 1572868
  253.6 15.2 %collective-permute-start.1 = (bf16[2,1024,128]{2,1,0:T(8,128)(2,1)S(1)}, bf16[2,1024,128]{2,1,0:T(8,128)(2,1)S(1)}, u32[]{:S(2)}, u32[]{:S(2)}) collective-permute-start(bf16[2,1024,128]{2,1,0:T(8,128)(2,1)S(1)} %collective-permute-done), channel_id=1, source_target_pairs={{15,0},{0,1},{1,2},{2,3},{3,4},{4,5},{5,6},{6,7},{7,8},{8,9},{9,10... | collective-permute-start | bytes 1572872 | tf_op jit(solution)/shard_map/ppermute | solution.py:20
  268.8 26.8 %copy-start.9 = (bf16[2,1024,128]{2,1,0:T(8,128)(2,1)}, bf16[2,1024,128]{2,1,0:T(8,128)(2,1)S(1)}, u32[]{:S(2)}) copy-start(bf16[2,1024,128]{2,1,0:T(8,128)(2,1)S(1)} %collective-permute-done.1) | copy-start | bytes 1572868
  268.8 14.3 %collective-permute-start.2 = (bf16[2,1024,128]{2,1,0:T(8,128)(2,1)S(1)}, bf16[2,1024,128]{2,1,0:T(8,128)(2,1)S(1)}, u32[]{:S(2)}, u32[]{:S(2)}) collective-permute-start(bf16[2,1024,128]{2,1,0:T(8,128)(2,1)S(1)} %collective-permute-done.1), channel_id=1, source_target_pairs={{15,0},{0,1},{1,2},{2,3},{3,4},{4,5},{5,6},{6,7},{7,8},{8,9},{9,10... | collective-permute-start | bytes 1572872 | tf_op jit(solution)/shard_map/ppermute | solution.py:20
  283.2 13.2 %copy-start.11 = (bf16[2,1024,128]{2,1,0:T(8,128)(2,1)}, bf16[2,1024,128]{2,1,0:T(8,128)(2,1)S(1)}, u32[]{:S(2)}) copy-start(bf16[2,1024,128]{2,1,0:T(8,128)(2,1)S(1)} %collective-permute-done.2) | copy-start | bytes 1572868
  297.9 2.8 copy-start.2
  297.9 2.8 copy-start.3
  300.8 5.0 %copy-start.4 = (f32[1024,512]{0,1:T(8,128)S(1)}, f32[1024,512]{0,1:T(8,128)}, u32[]{:S(2)}) copy-start(f32[1024,512]{0,1:T(8,128)} %fusion.125) | copy-start | bytes 6291460
  305.8 1.6 copy-start.5
  312.2 1.0 copy-start.8
  312.9 1.1 copy-start.10
  313.9 1.0 copy-start.12
  317.0 1.0 copy-start.6
  318.0 17.3 %copy-start.1 = (bf16[1,128,4096]{2,1,0:T(8,128)(2,1)S(1)}, bf16[1,128,4096]{2,1,0:T(8,128)(2,1)}, u32[]{:S(2)}) copy-start(bf16[1,128,4096]{2,1,0:T(8,128)(2,1)} %param.5) | copy-start | bytes 3145732
Sparse Core Ops, SparseCore 0:
  9.1 196.3 all-gather.1
where the time goes:
time: 343 us; the launch traced here: 342 us
  waiting for transfers between devices  237 us (69%)
  matrix products  40.2 us (12%)
  starting transfers between devices  16.1 us (5%)
  blocking collectives  15.7 us (5%)
  between operations  14 us (4%)
  other arithmetic  12.2 us (4%)
  local copies, waits for them, and re-layouts  7.27 us (2%)
    all_gather x1, waiting for transfers between devices, shards(): lax.all_gather(pair_weight, ('dp', 'blk'), axis=0, tiled=True)  188 us
    ppermute x3, waiting for transfers between devices, from_behind(): return lax.ppermute(block, axis, route)  35.9 us
    dot_general x16, matrix products, tile_scores(): lax.dot_general(query_rows, key_rows, (((1,), (1,)), ((), ())), preferred...  21.1 us
    all_to_all x1, blocking collectives, shards(): lax.all_to_all(block_output, 'ulysses', split_axis=0, concat_axis=1, tile...  15.7 us
    dot_general x16, matrix products, add_tile(): jnp.dot(weights.astype(jnp.bfloat16), value_rows, preferred_element_type=...  11 us
    reduce_sum x2, other arithmetic, add_tile(): denominator = denominator + jnp.sum(weights, axis=1)  9.41 us
    dot_general x1, matrix products, shards(): jnp.dot(inputs_local, lax.all_gather(pair_weight, ('dp', 'blk'), axis=0,...  8.1 us
  transfers between devices with their start and end apart: 7, of which 6 were waited for; matrix products, arithmetic and copies ran while one was open for 7% of the time, Pallas kernels for 0%

commit v1 on v0

v1 whole, which is shorter than its diff:
```python
import math

import jax
import jax.numpy as jnp
from jax import lax
from jax.experimental import pallas as pl
from jax.experimental.pallas import tpu as pltpu
from jax.sharding import PartitionSpec as P

KVH = 8
HD = 128
QH = 16
STEPS = 3
UL = 8
NZ = 8
LOG_BASE = math.log(500000.0)
MESH = pl.DeviceIdType.MESH
SCALE2 = (1.0 / math.sqrt(HD)) * math.log2(math.e)
NEG = -1.0e30
FAR = 2.0e30


def wrap(value, size):
    return lax.rem(value + size, size)


def kernel(
    order_ref, hid, qry, pw, cos_ref, sin_ref, out,
    wbuf, hbuf, qbuf, qrot, kvbuf, m_ref, l_ref, acc_ref, obuf,
    ssem, rsem, lsem,
):
    dp = lax.axis_index("dp")
    u = lax.axis_index("ulysses")
    blk = lax.axis_index("blk")
    core = lax.rem(u, 2)
    x = u // 2
    yh = blk // NZ
    z = lax.rem(blk, NZ)
    y = yh * 2 + dp

    counter = [0]

    def take(n):
        base = counter[0]
        counter[0] += n
        return base

    def ul(index):
        return {"ulysses": index}

    def ydev(offset):
        other = lax.rem(y + offset, 4)
        return other, {"dp": lax.rem(other, 2), "blk": (other // 2) * NZ + z}

    def zdev(offset):
        return {"blk": yh * NZ + wrap(z + offset, NZ)}

    u_plus, u_minus = lax.rem(u + 2, UL), lax.rem(u + UL - 2, UL)
    u_far = lax.rem(u + 4, UL)
    partner = u + 1 - 2 * core
    next_blk = {"blk": lax.rem(blk + 1, 16)}
    prev_blk = {"blk": lax.rem(blk + 15, 16)}

    def rcopy(src, dst, index, device):
        return pltpu.make_async_remote_copy(
            src_ref=src, dst_ref=dst, send_sem=ssem.at[index], recv_sem=rsem.at[index],
            device_id=device, device_id_type=MESH,
        )

    sends = []

    def send(src, dst, index, device):
        copy = rcopy(src, dst, index, device)
        copy.start()
        sends.append(copy)

    def arrive(dst, index):
        rcopy(dst, dst, index, ul(partner)).wait_recv()

    barrier = pltpu.get_barrier_semaphore()
    greet = [ul(lax.rem(u + o, UL)) for o in range(1, UL)]
    greet += [ydev(o)[1] for o in range(1, 4)]
    greet += [zdev(1), zdev(-1), next_blk, prev_blk]
    for device in greet:
        pl.semaphore_signal(barrier, inc=1, device_id=device, device_id_type=MESH)
    pl.semaphore_wait(barrier, len(greet))

    own_k = pw.at[:, pl.ds(pl.multiple_of(u * HD, HD), HD)]
    own_v = pw.at[:, pl.ds(pl.multiple_of(KVH * HD + u * HD, HD), HD)]
    WB = (take(4), take(3))
    WAY = take(3)
    WAZ = (take(8), take(6))
    WBY = take(4)
    HX, HR, HP = take(4), take(2), take(7)
    QX = take(7)
    KV = take(12)
    OX = take(7)

    def vpiece(yy, zz):
        return wbuf.at[lax.rem(yy, 2), yy // 2, zz, :, pl.ds(HD, HD)]

    def kpiece(yy, zz):
        return wbuf.at[lax.rem(yy, 2), yy // 2, zz, :, pl.ds(0, HD)]

    def kbundle(g, zz):
        return wbuf.at[g, :, zz, :, pl.ds(0, HD)]

    def vbundle(yy, lo, size):
        return wbuf.at[lax.rem(yy, 2), yy // 2, pl.ds(lo, size), :, pl.ds(HD, HD)]

    send(own_v, vpiece(y, z), WB[0], zdev(1))
    send(own_v, vpiece(y, z), WB[1], zdev(-1))
    for o in range(1, 4):
        send(own_k, kpiece(y, z), WAY + o - 1, ydev(o)[1])

    local = [
        pltpu.make_async_copy(own_k, kpiece(y, z), lsem.at[0]),
        pltpu.make_async_copy(own_v, vpiece(y, z), lsem.at[1]),
        pltpu.make_async_copy(hid, hbuf.at[u], lsem.at[2]),
        pltpu.make_async_copy(
            qry.at[:, pl.ds(pl.multiple_of(u * 2 * HD, HD), 2 * HD)], qbuf.at[u], lsem.at[3]
        ),
    ]
    for copy in local:
        copy.start()

    send(hid, hbuf.at[u], HP, ul(partner))
    for half in range(2):
        rows = pl.ds(half * 64, 64)
        send(hid.at[rows], hbuf.at[u, rows], HX + half, ul(u_plus))
        send(hid.at[rows], hbuf.at[u, rows], HX + 2 + half, ul(u_minus))
    for o in range(1, UL):
        peer = lax.rem(u + o, UL)
        send(
            qry.at[:, pl.ds(pl.multiple_of(peer * 2 * HD, HD), 2 * HD)],
            qbuf.at[u], QX + o - 1, ul(peer),
        )

    hops = (4, 3)
    steps = (-1, 1)

    def v_hop(h):
        for way in range(2):
            if h <= hops[way]:
                zz = wrap(z + steps[way] * h, NZ)
                arrive(vpiece(y, zz), WB[way] + h - 1)
                if h < hops[way]:
                    send(vpiece(y, zz), vpiece(y, zz), WB[way] + h, zdev(-steps[way]))

    def k_hop(h):
        for way in range(2):
            for g in range(2):
                if h == 0 or h <= hops[way]:
                    zz = wrap(z + steps[way] * h, NZ)
                    if h > 0:
                        arrive(kbundle(g, zz), WAZ[way] + 2 * (h - 1) + g)
                    if h < hops[way]:
                        send(kbundle(g, zz), kbundle(g, zz), WAZ[way] + 2 * h + g, zdev(-steps[way]))

    v_hop(1)
    local[0].wait()
    for o in range(1, 4):
        arrive(kpiece(lax.rem(y + 4 - o, 4), z), WAY + o - 1)
    k_hop(0)
    v_hop(2)
    v_hop(3)
    k_hop(1)
    v_hop(4)
    local[1].wait()
    y_up, y_down, y_far = lax.rem(y + 1, 4), lax.rem(y + 3, 4), lax.rem(y + 2, 4)
    send(vbundle(y, 0, NZ), vbundle(y, 0, NZ), WBY, ydev(1)[1])
    send(vbundle(y, 0, NZ), vbundle(y, 0, NZ), WBY + 1, ydev(3)[1])
    k_hop(2)
    arrive(vbundle(y_down, 0, NZ), WBY)
    send(vbundle(y_down, 0, 4), vbundle(y_down, 0, 4), WBY + 2, ydev(1)[1])
    arrive(vbundle(y_up, 0, NZ), WBY + 1)
    send(vbundle(y_up, 4, 4), vbundle(y_up, 4, 4), WBY + 3, ydev(3)[1])
    k_hop(3)
    k_hop(4)
    arrive(vbundle(y_far, 0, 4), WBY + 2)
    arrive(vbundle(y_far, 4, 4), WBY + 3)

    def project(xc):
        rows = hbuf[pl.ds(2 * xc, 2)].reshape(256, 4096)
        weight = wbuf[...].reshape(4096, 2 * HD)
        result = jnp.dot(rows, weight, preferred_element_type=jnp.float32)
        at = pl.ds(pl.multiple_of(xc * 256, 256), 256)
        key = result[:, :HD]
        key = key * cos_ref[at, :] + pltpu.roll(key, HD // 2, 1) * sin_ref[at, :]
        kvbuf[0, pl.ds(2 * xc, 2), 0] = key.astype(jnp.bfloat16).reshape(2, 128, HD)
        kvbuf[0, pl.ds(2 * xc, 2), 1] = result[:, HD:].astype(jnp.bfloat16).reshape(2, 128, HD)

    chunk = (x, x + 1 - 2 * lax.rem(x, 2), 3 - x, lax.rem(x + 2, 4))

    def kv_region(d, c):
        return kvbuf.at[d, pl.ds(2 * chunk[c], 2)]

    def pass_on(d, c):
        if d > 1:
            arrive(kv_region(d - 1, c), KV + (d - 2) * 4 + c)
        send(kv_region(d - 1, c), kv_region(d, c), KV + (d - 1) * 4 + c, next_blk)

    local[2].wait()
    arrive(hbuf.at[partner], HP)
    project(chunk[0])
    pass_on(1, 0)

    def half_rows(slot, half):
        return hbuf.at[slot, pl.ds(half * 64, 64)]

    for half in range(2):
        arrive(half_rows(u_minus, half), HX + half)
        if half == 0:
            send(half_rows(u_minus, 0), half_rows(u_minus, 0), HR, ul(u_plus))
        send(half_rows(u_minus, half), half_rows(u_minus, half), HP + 1 + half, ul(partner))
        arrive(half_rows(u_plus, half), HX + 2 + half)
        if half == 1:
            send(half_rows(u_plus, 1), half_rows(u_plus, 1), HR + 1, ul(u_minus))
        send(half_rows(u_plus, half), half_rows(u_plus, half), HP + 3 + half, ul(partner))
        pass_on(2 + half, 0)

    p_minus, p_plus, p_far = (lax.rem(partner + UL - 2, UL), lax.rem(partner + 2, UL), lax.rem(partner + 4, UL))
    for half in range(2):
        arrive(half_rows(p_minus, half), HP + 1 + half)
        arrive(half_rows(p_plus, half), HP + 3 + half)
    project(chunk[1])
    pass_on(1, 1)
    project(chunk[2])
    pass_on(1, 2)

    m_ref[...] = jnp.full_like(m_ref, NEG)
    l_ref[...] = jnp.zeros_like(l_ref)
    acc_ref[...] = jnp.zeros_like(acc_ref)
    local[3].wait()
    for o in range(1, UL):
        arrive(qbuf.at[lax.rem(u + UL - o, UL)], QX + o - 1)

    def rope_slice(s, carry):
        at = pl.ds(pl.multiple_of(s * 128, 128), 128)
        cosine = cos_ref[at, :]
        sine = sin_ref[at, :]
        for head in range(2):
            q = qbuf[s, :, head * HD : (head + 1) * HD].astype(jnp.float32)
            q = q * cosine + pltpu.roll(q, HD // 2, 1) * sine
            place = (s // 4) * 4 + head * 2 + lax.rem(s, 4) // 2
            qrot[place, pl.ds(pl.multiple_of(lax.rem(s, 2) * 128, 128), 128)] = q.astype(jnp.bfloat16)
        return carry

    lax.fori_loop(0, UL, rope_slice, 0)

    def attend(qh, d, kh):
        source = lax.rem(blk + 16 - d, 16)
        key_order = order_ref[0, 2 * source + kh]
        query_order = order_ref[0, 2 * blk + qh]
        shut = key_order > query_order
        low = jnp.where(shut, -FAR, 0.0)
        lift = jnp.where(shut, FAR, 0.0)

        def rows_of(i, carry):
            place = qh * 4 + i
            keys = kvbuf[d, pl.ds(4 * kh, 4), 0].reshape(512, HD)
            values = kvbuf[d, pl.ds(4 * kh, 4), 1].reshape(512, HD)
            score = lax.dot_general(
                qrot[place], keys, (((1,), (1,)), ((), ())), preferred_element_type=jnp.float32
            )
            if d == 0:
                first = lax.rem(i, 2) * 256 + 1024 * lax.rem(qh + kh, 2)
                row = lax.broadcasted_iota(jnp.int32, score.shape, 0) + first
                column = lax.broadcasted_iota(jnp.int32, score.shape, 1)
                score = jnp.where(row >= column, score, NEG)
            old = m_ref[place]
            top = jnp.max(score, axis=1, keepdims=True) + low
            new = jnp.maximum(old, top)
            base = new + lift
            weight = jnp.exp2((score - jnp.tile(base, (1, 4))) * SCALE2)
            shrink = jnp.exp2((old - new) * SCALE2)
            part = (weight[:, :128] + weight[:, 128:256]) + (weight[:, 256:384] + weight[:, 384:])
            l_ref[place] = l_ref[place] * shrink + part
            acc_ref[place] = acc_ref[place] * shrink + jnp.dot(
                weight.astype(jnp.bfloat16), values, preferred_element_type=jnp.float32
            )
            m_ref[place] = new
            return carry

        lax.fori_loop(0, 4, rows_of, 0)

    own = x // 2
    oth = 1 - own

    attend(0, 0, own)
    pass_on(2, 1)
    attend(1, 0, own)
    pass_on(2, 2)
    attend(0, 1, own)
    pass_on(3, 1)
    attend(1, 1, own)
    pass_on(3, 2)
    arrive(half_rows(u_far, 0), HR)
    send(half_rows(u_far, 0), half_rows(u_far, 0), HP + 5, ul(partner))
    arrive(half_rows(u_far, 1), HR + 1)
    send(half_rows(u_far, 1), half_rows(u_far, 1), HP + 6, ul(partner))
    attend(0, 2, own)
    for half in range(2):
        arrive(half_rows(p_far, half), HP + 5 + half)
    project(chunk[3])
    pass_on(1, 3)
    attend(1, 2, own)
    attend(0, 0, oth)
    pass_on(2, 3)
    attend(1, 0, oth)
    arrive(kv_region(3, 0), KV + 8)
    arrive(kv_region(3, 1), KV + 9)
    attend(0, 3, own)
    pass_on(3, 3)
    attend(1, 3, own)
    for qh in range(2):
        attend(qh, 1, oth)
    for qh in range(2):
        attend(qh, 2, oth)
    arrive(kv_region(3, 2), KV + 10)
    arrive(kv_region(3, 3), KV + 11)
    for qh in range(2):
        attend(qh, 3, oth)

    for qh in range(2):
        for head in range(2):
            for sub in range(2):
                place = qh * 4 + head * 2 + sub
                total = jnp.sum(l_ref[place], axis=1, keepdims=True)
                value = (acc_ref[place] / total).astype(jnp.bfloat16)
                obuf[qh * 4 + sub * 2 : qh * 4 + sub * 2 + 2, :, head * HD : (head + 1) * HD] = value.reshape(2, 128, HD)
    own_out = pltpu.make_async_copy(
        obuf.at[u], out.at[:, pl.ds(pl.multiple_of(u * 2 * HD, HD), 2 * HD)], lsem.at[4]
    )
    own_out.start()
    here = out.at[:, pl.ds(pl.multiple_of(u * 2 * HD, HD), 2 * HD)]
    for o in range(1, UL):
        peer = lax.rem(u + o, UL)
        send(obuf.at[peer], here, OX + o - 1, ul(peer))
    own_out.wait()
    for o in range(1, UL):
        source = lax.rem(u + UL - o, UL)
        arrive(out.at[:, pl.ds(pl.multiple_of(source * 2 * HD, HD), 2 * HD)], OX + o - 1)
    for copy in sends:
        copy.wait_send()


def shards(hidden_in, queries, pair_weight, span_order, yarn_divisor):
    blk = lax.axis_index("blk")
    order_row = span_order[0]
    spans = lax.dynamic_slice(order_row, (2 * blk,), (2,))
    pos = (spans[:, None] * 512 + jnp.arange(512, dtype=jnp.int32)[None, :]).reshape(1024)
    scaled = 2.0 * jnp.arange(HD // 2, dtype=jnp.float32) / HD
    inverse = jnp.exp(-LOG_BASE * scaled) / yarn_divisor.astype(jnp.float32)
    angle = pos.astype(jnp.float32)[:, None] * inverse[None, :]
    cosine = jnp.cos(angle)
    sine = jnp.sin(angle)
    cosine = jnp.concatenate([cosine, cosine], axis=1)
    sine = jnp.concatenate([-sine, sine], axis=1)
    anywhere = pl.BlockSpec(memory_space=pl.ANY)
    vmem = pl.BlockSpec(memory_space=pltpu.VMEM)
    out = pl.pallas_call(
        kernel,
        out_shape=jax.ShapeDtypeStruct((128, QH * HD), jnp.bfloat16),
        in_specs=[pl.BlockSpec(memory_space=pltpu.SMEM), anywhere, anywhere, anywhere, vmem, vmem],
        out_specs=anywhere,
        scratch_shapes=[
            pltpu.VMEM((2, 2, NZ, 128, 2 * HD), jnp.bfloat16),
            pltpu.VMEM((UL, 128, 4096), jnp.bfloat16),
            pltpu.VMEM((UL, 128, 2 * HD), jnp.bfloat16),
            pltpu.VMEM((8, 256, HD), jnp.bfloat16),
            pltpu.VMEM((STEPS + 1, UL, 2, 128, HD), jnp.bfloat16),
            pltpu.VMEM((8, 256, HD), jnp.float32),
            pltpu.VMEM((8, 256, HD), jnp.float32),
            pltpu.VMEM((8, 256, HD), jnp.float32),
            pltpu.VMEM((UL, 128, 2 * HD), jnp.bfloat16),
            pltpu.SemaphoreType.DMA((80,)),
            pltpu.SemaphoreType.DMA((80,)),
            pltpu.SemaphoreType.DMA((5,)),
        ],
        compiler_params=pltpu.CompilerParams(
            collective_id=0, has_side_effects=True, vmem_limit_bytes=48 * 1024 * 1024
        ),
    )(span_order, hidden_in[0], queries[0], pair_weight, cosine, sine)
    return out[None]


def solution(mesh):
    return jax.shard_map(
        shards,
        mesh=mesh,
        in_specs=(
            P("dp", ("blk", "ulysses"), None),
            P("dp", ("blk", "ulysses"), None),
            P(("dp", "blk"), None),
            P("dp", None),
            P(),
        ),
        out_specs=P("dp", ("blk", "ulysses"), None),
        check_vma=False,
    )
```

time: 343 us -> 105 us (0.31)
  waiting for transfers between devices: 237 us -> 0 us
  Pallas kernels: 0 us -> 99.6 us
  matrix products: 40.2 us -> 0 us
  starting transfers between devices: 16.1 us -> 0 us
  blocking collectives: 15.7 us -> 0 us
  between operations: 14 us -> 0.05 us
  other arithmetic: 12.2 us -> 2.4 us
  local copies, waits for them, and re-layouts: 7.27 us -> 3.26 us
    all_gather x1 -> x0, waiting for transfers between devices: 188 us -> none  [shards(): lax.all_gather(pair_weight, ('dp', 'blk'), axis=0, tiled=True)]
    pallas_call x0 -> x1, Pallas kernels: none -> 99.6 us  [shards(): pl.pallas_call(kernel, out_shape=jax.ShapeDtypeStruct((128, QH * HD), jnp...]
    dot_general x33 -> x0, matrix products: 40.2 us -> none  [the longest x16 21.1 us: tile_scores(): lax.dot_general(query_rows, key_rows, (((1,), (1,)), ((), ())), preferred...]
    ppermute x3 -> x0, waiting for transfers between devices: 35.9 us -> none  [from_behind(): return lax.ppermute(block, axis, route)]
    all_to_all x3 -> x0, starting transfers between devices: 16 us -> none  [the longest x1 6.6 us: shards(): lax.all_to_all(rotated_queries, 'ulysses', split_axis=1, concat_axis=0, t...]
    all_to_all x1 -> x0, blocking collectives: 15.7 us -> none  [shards(): lax.all_to_all(block_output, 'ulysses', split_axis=0, concat_axis=1, tile...]
    all_to_all x3 -> x0, waiting for transfers between devices: 11.7 us -> none  [the longest x1 5.92 us: shards(): lax.all_to_all(token_values, 'ulysses', split_axis=1, concat_axis=0, tile...]
    reduce_sum x4 -> x0, other arithmetic: 9.68 us -> none  [the longest x2 9.41 us: add_tile(): denominator = denominator + jnp.sum(weights, axis=1)]
  transfers between devices with their start and end apart: 7 -> 0, of which waited for: 6 -> 0; matrix products, arithmetic and copies ran while one was open for 7% -> 0% of each run, Pallas kernels for 0% -> 0%
where the time goes in v1:
time: 105 us
  Pallas kernels  99.6 us (95%)
  local copies, waits for them, and re-layouts  3.26 us (3%)
  other arithmetic  2.4 us (2%)
    pallas_call x1, Pallas kernels, shards(): pl.pallas_call(kernel, out_shape=jax.ShapeDtypeStruct((128, QH * HD), jnp...  99.6 us
    unnamed x12, local copies, waits for them, and re-layouts  3.26 us

profile of v1, /device:TPU:1, one launch (start us, length us, event | category | flops | bytes accessed | tf_op | source)
XLA Modules:
  0.0 105.3 jit_solution(9703652706249266958)
XLA Ops:
  0.0 0.0 copy-start.3
  0.0 0.7 copy-done.3
  0.7 0.1 multiply_bitcast_fusion
  0.7 0.0 copy-start.4
  0.7 0.7 copy-done.4
  1.4 0.1 convert_bitcast_fusion
  1.5 1.9 %fusion = (f32[1024,64]{1,0:T(8,128)S(1)}, f32[1024,64]{1,0:T(8,128)S(1)}, f32[1024,64]{1,0:T(8,128)S(1)}) fusion(f32[64]{0:T(128)S(1)} %convert_divide_fusion, f32[1024]{0:T(1024)S(1)} %bitcast.11), kind=kLoop, calls=%fused_computation.4 | loop fusion | flops 131072 | bytes 790784 | tf_op jit(solution)/shard_map/neg | solution.py:359
  3.4 0.0 copy-start
  3.4 0.0 copy-start.1
  3.4 0.0 copy-start.2
  3.4 0.3 pad_maximum_fusion
  3.8 0.8 copy-done
  4.6 0.1 copy-done.1
  4.7 0.2 copy-done.2
  4.9 99.6 %shard_map.55 = bf16[128,2048]{1,0:T(8,128)(2,1)S(1)} custom-call(s32[1,32]{1,0:T(1,128)S(1)} %copy-done.3, bf16[128,4096]{1,0:T(8,128)(2,1)S(1)} %bitcast.9, bf16[128,2048]{1,0:T(8,128)(2,1)S(1)} %bitcast.10, bf16[128,2048]{1,0:T(8,128)(2,1)S(1)} %copy-done.2, f32[1024,128]{1,0:T(8,128)S(1)} %get-tuple-element.8.cos_ref, ...), custom_call_target="tpu_custom_call" | custom-call | tf_op jit(solution)/shard_map/pallas_call | solution.py:362
  104.6 0.8 copy.8
  (2 shorter events, 0.0 us)
Async XLA Ops:
  0.0 0.7 copy-start.3
  0.7 0.7 copy-start.4
  3.4 1.2 %copy-start = (bf16[1,128,4096]{2,1,0:T(8,128)(2,1)S(1)}, bf16[1,128,4096]{2,1,0:T(8,128)(2,1)}, u32[]{:S(2)}) copy-start(bf16[1,128,4096]{2,1,0:T(8,128)(2,1)} %param.5) | copy-start | bytes 3145732
  3.4 1.3 %copy-start.1 = (bf16[1,128,2048]{2,1,0:T(8,128)(2,1)S(1)}, bf16[1,128,2048]{2,1,0:T(8,128)(2,1)}, u32[]{:S(2)}) copy-start(bf16[1,128,2048]{2,1,0:T(8,128)(2,1)} %param.6) | copy-start | bytes 1572868
  3.4 1.5 %copy-start.2 = (bf16[128,2048]{1,0:T(8,128)(2,1)S(1)}, bf16[128,2048]{1,0:T(8,128)(2,1)}, u32[]{:S(2)}) copy-start(bf16[128,2048]{1,0:T(8,128)(2,1)} %pw.1) | copy-start | bytes 1572868

commit v2 on v1

v2 whole, which is shorter than its diff:
```python
import math

import jax
import jax.numpy as jnp
from jax import lax
from jax.experimental import pallas as pl
from jax.experimental.pallas import tpu as pltpu
from jax.sharding import PartitionSpec as P
import numpy as np

KVH = 8
HD = 128
QH = 16
STEPS = 3
UL = 8
NZ = 8
LOG_BASE = math.log(500000.0)
MESH = pl.DeviceIdType.MESH
SCALE2 = (1.0 / math.sqrt(HD)) * math.log2(math.e)
NEG = -1.0e30
FREQUENCIES = [
    float(np.exp(np.float32(-LOG_BASE) * (np.float32(2 * f) / np.float32(HD)), dtype=np.float32)) for f in range(HD // 2)
]
FAR = 2.0e30


def wrap(value, size):
    return lax.rem(value + size, size)


def kernel(
    order_hbm, divisor_hbm, hid, qry, pw, out,
    order_ref, divisor_ref, cos_ref, sin_ref, wbuf, hbuf, qbuf, qrot, kvbuf, m_ref, l_ref, acc_ref, obuf,
    ssem, rsem, lsem,
):
    dp = lax.axis_index("dp")
    u = lax.axis_index("ulysses")
    blk = lax.axis_index("blk")
    core = lax.rem(u, 2)
    other_core = 1 - core
    x = u // 2
    yh = blk // NZ
    z = lax.rem(blk, NZ)
    y = yh * 2 + dp

    counter = [0]

    def take(n):
        base = counter[0]
        counter[0] += n
        return base

    def ul(index):
        return {"ulysses": index}

    def chip(offset, on_core):
        return ul(2 * lax.rem(x + offset, 4) + on_core)

    def ydev(offset):
        other = lax.rem(y + offset, 4)
        return {"dp": lax.rem(other, 2), "blk": (other // 2) * NZ + z}

    def zdev(offset):
        return {"blk": yh * NZ + wrap(z + offset, NZ)}

    x_plus, x_far, x_minus = lax.rem(x + 1, 4), lax.rem(x + 2, 4), lax.rem(x + 3, 4)
    partner = u + 1 - 2 * core
    next_blk = {"blk": lax.rem(blk + 1, 16)}
    prev_blk = {"blk": lax.rem(blk + 15, 16)}

    def rcopy(src, dst, index, device):
        return pltpu.make_async_remote_copy(
            src_ref=src, dst_ref=dst, send_sem=ssem.at[index], recv_sem=rsem.at[index],
            device_id=device, device_id_type=MESH,
        )

    sends = []

    def send(src, dst, index, device):
        copy = rcopy(src, dst, index, device)
        copy.start()
        sends.append(copy)

    def arrive(dst, index):
        rcopy(dst, dst, index, ul(partner)).wait_recv()

    own_k = pw.at[:, pl.ds(pl.multiple_of(u * HD, HD), HD)]
    own_v = pw.at[:, pl.ds(pl.multiple_of(KVH * HD + u * HD, HD), HD)]
    WB = (take(4), take(3))
    WAY = take(3)
    WAZ = (take(8), take(8))
    WBY = (take(8), take(8))
    WBF = take(8)
    HX, HR, HP = take(4), take(2), take(8)
    QX = take(7)
    KV = take(24)
    OX = take(7)

    def vpiece(yy, zz):
        return wbuf.at[lax.rem(yy, 2), yy // 2, zz, :, pl.ds(HD, HD)]

    def kpiece(yy, zz):
        return wbuf.at[lax.rem(yy, 2), yy // 2, zz, :, pl.ds(0, HD)]

    def kbundle(g, zz):
        return wbuf.at[g, :, zz, :, pl.ds(0, HD)]

    def hid_half(a):
        return hid.at[pl.ds(a * 64, 64)]

    def qry_for(index):
        return qry.at[:, pl.ds(pl.multiple_of(index * 2 * HD, HD), 2 * HD)]

    local = [
        pltpu.make_async_copy(own_k, kpiece(y, z), lsem.at[0]),
        pltpu.make_async_copy(own_v, vpiece(y, z), lsem.at[1]),
        pltpu.make_async_copy(hid_half(0), hbuf.at[x, 0, core], lsem.at[2]),
        pltpu.make_async_copy(hid_half(1), hbuf.at[x, 1, core], lsem.at[3]),
        pltpu.make_async_copy(qry_for(u), qbuf.at[u], lsem.at[4]),
        pltpu.make_async_copy(order_hbm, order_ref, lsem.at[6]),
        pltpu.make_async_copy(divisor_hbm, divisor_ref, lsem.at[7]),
    ]
    for copy in local:
        copy.start()

    barrier = pltpu.get_barrier_semaphore()
    greet = [ul(lax.rem(u + o, UL)) for o in range(1, UL)]
    greet += [ydev(o) for o in range(1, 4)]
    greet += [zdev(1), zdev(-1), next_blk, prev_blk]
    for device in greet:
        pl.semaphore_signal(barrier, inc=1, device_id=device, device_id_type=MESH)
    pl.semaphore_wait(barrier, len(greet))

    send(own_v, vpiece(y, z), WB[0], zdev(1))
    send(own_v, vpiece(y, z), WB[1], zdev(-1))
    for o in (2, 1, 3):
        send(own_k, kpiece(y, z), WAY + o - 1, ydev(o))
    for a in range(2):
        send(hid_half(a), hbuf.at[x, a, core], HX + a, chip(1, core))
        send(hid_half(a), hbuf.at[x, a, core], HX + 2 + a, chip(3, core))
        send(hid_half(a), hbuf.at[x, a, core], HP + a, ul(partner))
        if a == 0:
            for o in range(1, UL):
                peer = lax.rem(u + o, UL)
                send(qry_for(peer), qbuf.at[u], QX + o - 1, ul(peer))

    spots = {0: 0, -1: 1, 1: 2, -2: 3, 2: 4, -3: 5, 3: 6, -4: 7}
    y_up, y_down, y_far = lax.rem(y + 1, 4), lax.rem(y + 3, 4), lax.rem(y + 2, 4)

    def v_spread(offset, source=None):
        zz = wrap(z + offset, NZ)
        src = vpiece(y, zz) if source is None else source
        send(src, vpiece(y, zz), WBY[0] + spots[offset], ydev(1))
        send(src, vpiece(y, zz), WBY[1] + spots[offset], ydev(3))

    def v_hop(h):
        for way, step in ((0, -1), (1, 1)):
            if h <= (4, 3)[way]:
                zz = wrap(z + step * h, NZ)
                arrive(vpiece(y, zz), WB[way] + h - 1)
                if h < (4, 3)[way]:
                    send(vpiece(y, zz), vpiece(y, zz), WB[way] + h, zdev(-step))
                v_spread(step * h)

    def v_across(*offsets):
        for offset in offsets:
            zz = wrap(z + offset, NZ)
            spot = spots[offset]
            arrive(vpiece(y_down, zz), WBY[0] + spot)
            if spot % 2 == 0:
                send(vpiece(y_down, zz), vpiece(y_down, zz), WBF + spot, ydev(1))
            arrive(vpiece(y_up, zz), WBY[1] + spot)
            if spot % 2 == 1:
                send(vpiece(y_up, zz), vpiece(y_up, zz), WBF + spot, ydev(3))

    def k_hop(h):
        for g in range(2):
            for way, step in ((0, -1), (1, 1)):
                last = 4 if g == way else 3
                if h <= last:
                    zz = wrap(z + step * h, NZ)
                    if h > 0:
                        arrive(kbundle(g, zz), WAZ[way] + 2 * (h - 1) + g)
                    if h < last:
                        send(kbundle(g, zz), kbundle(g, zz), WAZ[way] + 2 * h + g, zdev(-step))

    v_spread(0, own_v)
    v_hop(1)
    local[0].wait()
    for o in range(1, 4):
        arrive(kpiece(lax.rem(y + 4 - o, 4), z), WAY + o - 1)
    k_hop(0)
    v_hop(2)
    v_across(0)
    v_hop(3)
    v_across(-1, 1)
    k_hop(1)
    v_hop(4)
    v_across(-2, 2)
    k_hop(2)

    local[5].wait()
    local[6].wait()
    lane64 = lax.broadcasted_iota(jnp.int32, (1, HD // 2), 1)
    inverse = jnp.zeros((1, HD // 2), jnp.float32)
    for f, value in enumerate(FREQUENCIES):
        inverse = jnp.where(lane64 == f, value, inverse)
    inverse = inverse / divisor_ref[...].astype(jnp.float32)
    inverse = jnp.concatenate([inverse, inverse], axis=1)

    def table(i, carry):
        start = order_ref[0, 2 * blk + i // 4] * 512 + lax.rem(i, 4) * 128
        pos = lax.broadcasted_iota(jnp.int32, (128, HD), 0) + start
        angle = pos.astype(jnp.float32) * inverse
        lane = lax.broadcasted_iota(jnp.int32, (128, HD), 1)
        sine = jnp.sin(angle)
        at = pl.ds(pl.multiple_of(i * 128, 128), 128)
        cos_ref[at, :] = jnp.cos(angle)
        sin_ref[at, :] = jnp.where(lane < HD // 2, -sine, sine)
        return carry

    lax.fori_loop(0, UL, table, 0)
    m_ref[...] = jnp.full_like(m_ref, NEG)
    l_ref[...] = jnp.zeros_like(l_ref)
    acc_ref[...] = jnp.zeros_like(acc_ref)

    v_across(-3, 3)
    k_hop(3)
    v_across(-4)
    k_hop(4)
    for offset in spots:
        arrive(vpiece(y_far, wrap(z + offset, NZ)), WBF + spots[offset])
    local[1].wait()

    chunk = (x, x + 1 - 2 * lax.rem(x, 2), 3 - x, x_far)
    pieces = ((0, 0), (0, 1), (1, 0), (2, 0), (1, 1), (2, 1), (3, 0), (3, 1))

    def project(n):
        xc, a = chunk[pieces[n][0]], pieces[n][1]
        rows = hbuf[xc, a].reshape(128, 4096)
        weight = wbuf[...].reshape(4096, 2 * HD)
        result = jnp.dot(rows, weight, preferred_element_type=jnp.float32)
        key = result[:, :HD]
        turned = pltpu.roll(key, HD // 2, 1)
        for k in range(2):
            at = pl.ds(pl.multiple_of(xc * 256 + k * 128 + a * 64, 64), 64)
            part = slice(k * 64, (k + 1) * 64)
            rope = key[part] * cos_ref[at, :] + turned[part] * sin_ref[at, :]
            kvbuf[0, xc, a, 0, part] = rope.astype(jnp.bfloat16)
        kvbuf[0, xc, a, 1] = result[:, HD:].T.astype(jnp.bfloat16)
        pass_on(1, n)

    def kv_region(d, n):
        return kvbuf.at[d, chunk[pieces[n][0]], pieces[n][1]]

    def landed(d, n):
        arrive(kv_region(d, n), KV + (d - 1) * 8 + n)

    def pass_on(d, n):
        if d > 1:
            landed(d - 1, n)
        send(kv_region(d - 1, n), kv_region(d, n), KV + (d - 1) * 8 + n, next_blk)

    def side(a):
        arrive(hbuf.at[x_minus, a, core], HX + a)
        if a == 1:
            send(hbuf.at[x_minus, 1, core], hbuf.at[x_minus, 1, core], HR + 1, chip(1, core))
        send(hbuf.at[x_minus, a, core], hbuf.at[x_minus, a, core], HP + 2 + a, ul(partner))
        arrive(hbuf.at[x_plus, a, core], HX + 2 + a)
        if a == 0:
            send(hbuf.at[x_plus, 0, core], hbuf.at[x_plus, 0, core], HR, chip(3, core))
        send(hbuf.at[x_plus, a, core], hbuf.at[x_plus, a, core], HP + 4 + a, ul(partner))

    def side_partner(a):
        arrive(hbuf.at[x_minus, a, other_core], HP + 2 + a)
        arrive(hbuf.at[x_plus, a, other_core], HP + 4 + a)

    for a in range(2):
        local[2 + a].wait()
        arrive(hbuf.at[x, a, other_core], HP + a)
        project(a)
    side(0)
    side_partner(0)
    project(2)
    project(3)

    local[4].wait()
    for o in range(1, UL):
        arrive(qbuf.at[lax.rem(u + UL - o, UL)], QX + o - 1)

    def rope_slice(s, carry):
        at = pl.ds(pl.multiple_of(s * 128, 128), 128)
        cosine = cos_ref[at, :]
        sine = sin_ref[at, :]
        for head in range(2):
            q = qbuf[s, :, head * HD : (head + 1) * HD].astype(jnp.float32)
            q = q * cosine + pltpu.roll(q, HD // 2, 1) * sine
            place = (s // 2) * 2 + head
            qrot[place, pl.ds(pl.multiple_of(lax.rem(s, 2) * 128, 128), 128)] = q.astype(jnp.bfloat16)
        return carry

    lax.fori_loop(0, UL, rope_slice, 0)

    def attend(first, count, *tiles):
        def one_chip(i, carry):
            j = first + i
            query_order = order_ref[0, 2 * blk + j // 2]
            lows, lifts = [], []
            for d, c in tiles:
                source = lax.rem(blk + 16 - d, 16)
                shut = order_ref[0, 2 * source + chunk[c] // 2] > query_order
                lows.append(jnp.where(shut, -FAR, 0.0))
                lifts.append(jnp.where(shut, FAR, 0.0))
            for head in range(2):
                place = 2 * j + head
                query = qrot[place]
                old = m_ref[place]
                new = old
                scores = []
                for (d, c), low in zip(tiles, lows):
                    keys = kvbuf[d, chunk[c], :, 0].reshape(256, HD)
                    score = lax.dot_general(
                        keys, query, (((1,), (1,)), ((), ())), preferred_element_type=jnp.float32
                    )
                    if d == 0:
                        row = lax.broadcasted_iota(jnp.int32, score.shape, 0)
                        shift = (lax.shift_right_logical(row, 6) & 1) - lax.shift_right_logical(row, 7)
                        key_at = row + 64 * shift + lax.rem(chunk[c], 2) * 256
                        apart = lax.rem(chunk[c] // 2 + j // 2, 2)
                        query_at = lax.broadcasted_iota(jnp.int32, score.shape, 1) + (
                            lax.rem(j, 2) * 256 + apart * 1024
                        )
                        score = jnp.where(query_at >= key_at, score, 4.0 * NEG)
                    scores.append(score)
                    new = jnp.maximum(new, jnp.max(score, axis=0, keepdims=True) + low)
                shrink = jnp.exp2((old - new) * SCALE2)
                total = l_ref[place] * shrink
                mixed = acc_ref[place] * shrink
                for (d, c), score, lift in zip(tiles, scores, lifts):
                    weight = jnp.exp2((score - (new + lift)) * SCALE2)
                    total = total + jnp.sum(weight.reshape(32, 8, 256), axis=0)
                    values = jnp.concatenate([kvbuf[d, chunk[c], 0, 1], kvbuf[d, chunk[c], 1, 1]], axis=1)
                    mixed = mixed + jnp.dot(
                        values, weight.astype(jnp.bfloat16), preferred_element_type=jnp.float32
                    )
                l_ref[place] = total
                acc_ref[place] = mixed
                m_ref[place] = new
            return carry

        lax.fori_loop(0, count, one_chip, 0)

    pass_on(2, 0)
    pass_on(2, 1)
    pass_on(2, 2)
    pass_on(2, 3)
    attend(0, 2, (0, 0), (1, 0))
    pass_on(3, 0)
    pass_on(3, 1)
    attend(2, 2, (0, 0), (1, 0))
    side(1)
    side_partner(1)
    project(4)
    project(5)
    pass_on(3, 2)
    pass_on(3, 3)
    attend(0, 4, (0, 1), (0, 2))
    pass_on(2, 4)
    pass_on(2, 5)
    landed(3, 0)
    landed(3, 1)
    attend(0, 2, (2, 0), (3, 0))
    pass_on(3, 4)
    pass_on(3, 5)
    attend(2, 2, (2, 0), (3, 0))
    arrive(hbuf.at[x_far, 0, core], HR)
    send(hbuf.at[x_far, 0, core], hbuf.at[x_far, 0, core], HP + 6, ul(partner))
    attend(0, 2, (1, 1), (1, 2))
    arrive(hbuf.at[x_far, 0, other_core], HP + 6)
    project(6)
    arrive(hbuf.at[x_far, 1, core], HR + 1)
    send(hbuf.at[x_far, 1, core], hbuf.at[x_far, 1, core], HP + 7, ul(partner))
    attend(2, 2, (1, 1), (1, 2))
    arrive(hbuf.at[x_far, 1, other_core], HP + 7)
    project(7)
    pass_on(2, 6)
    attend(0, 2, (2, 1), (2, 2))
    pass_on(2, 7)
    attend(2, 2, (2, 1), (2, 2))
    pass_on(3, 6)
    for n in (2, 4):
        landed(3, n)
    attend(0, 2, (0, 3), (3, 1))
    pass_on(3, 7)
    attend(2, 2, (0, 3), (3, 1))
    for n in (3, 5):
        landed(3, n)
    attend(0, 4, (3, 2), (1, 3))
    attend(0, 4, (2, 3))
    for n in (6, 7):
        landed(3, n)

    here = out.at[:, pl.ds(pl.multiple_of(u * 2 * HD, HD), 2 * HD)]
    own_out = pltpu.make_async_copy(obuf.at[u], here, lsem.at[5])
    for offset in (2, 1, 3, 0):
        j = lax.rem(x + offset, 4)
        attend(j, 1, (3, 3))
        for head in range(2):
            place = 2 * j + head
            total = jnp.sum(l_ref[place], axis=0, keepdims=True)
            value = (acc_ref[place] / total).T.astype(jnp.bfloat16)
            obuf[pl.ds(2 * j, 2), :, head * HD : (head + 1) * HD] = value.reshape(2, 128, HD)
        if offset:
            for k, to in enumerate((core, other_core)):
                send(obuf.at[2 * j + to], here, OX + (offset - 1) * 2 + k, ul(2 * j + to))
        else:
            own_out.start()
            send(obuf.at[partner], here, OX + 6, ul(partner))
    own_out.wait()

    def out_from(index):
        return out.at[:, pl.ds(pl.multiple_of(index * 2 * HD, HD), 2 * HD)]

    for offset in (2, 1, 3):
        for k, source_core in enumerate((core, other_core)):
            arrive(out_from(2 * lax.rem(x + 4 - offset, 4) + source_core), OX + (offset - 1) * 2 + k)
    arrive(out_from(partner), OX + 6)
    for copy in sends:
        copy.wait_send()


def shards(hidden_in, queries, pair_weight, span_order, yarn_divisor):
    anywhere = pl.BlockSpec(memory_space=pl.ANY)
    hbm = pl.BlockSpec(memory_space=pltpu.HBM)
    out = pl.pallas_call(
        kernel,
        out_shape=jax.ShapeDtypeStruct((128, QH * HD), jnp.bfloat16),
        in_specs=[
            hbm, hbm, hbm, hbm, hbm,
        ],
        out_specs=anywhere,
        scratch_shapes=[
            pltpu.SMEM((1, 32), jnp.int32),
            pltpu.VMEM((1, HD // 2), jnp.int32),
            pltpu.VMEM((1024, HD), jnp.float32),
            pltpu.VMEM((1024, HD), jnp.float32),
            pltpu.VMEM((2, 2, NZ, 128, 2 * HD), jnp.bfloat16),
            pltpu.VMEM((4, 2, 2, 64, 4096), jnp.bfloat16),
            pltpu.VMEM((UL, 128, 2 * HD), jnp.bfloat16),
            pltpu.VMEM((8, 256, HD), jnp.bfloat16),
            pltpu.VMEM((STEPS + 1, 4, 2, 2, 128, HD), jnp.bfloat16),
            pltpu.VMEM((8, 1, 256), jnp.float32),
            pltpu.VMEM((8, 8, 256), jnp.float32),
            pltpu.VMEM((8, HD, 256), jnp.float32),
            pltpu.VMEM((UL, 128, 2 * HD), jnp.bfloat16),
            pltpu.SemaphoreType.DMA((104,)),
            pltpu.SemaphoreType.DMA((104,)),
            pltpu.SemaphoreType.DMA((8,)),
        ],
        compiler_params=pltpu.CompilerParams(
            collective_id=0, has_side_effects=True, vmem_limit_bytes=61900 * 1024
        ),
    )(span_order, yarn_divisor[None, :], hidden_in[0], queries[0], pair_weight)
    return out[None]


def solution(mesh):
    return jax.shard_map(
        shards,
        mesh=mesh,
        in_specs=(
            P("dp", ("blk", "ulysses"), None),
            P("dp", ("blk", "ulysses"), None),
            P(("dp", "blk"), None),
            P("dp", None),
            P(),
        ),
        out_specs=P("dp", ("blk", "ulysses"), None),
        check_vma=False,
    )
```

time: 105 us -> 95.1 us (0.906)
  Pallas kernels: 99.6 us -> 93.1 us
  other arithmetic: 2.4 us -> 0 us
  local copies, waits for them, and re-layouts: 3.26 us -> 1.88 us
    pallas_call x1, Pallas kernels: 99.6 us -> 93.1 us  [shards(): pl.pallas_call(kernel, out_shape=jax.ShapeDtypeStruct((128, QH * HD), jnp...]
    neg x1 -> x0, other arithmetic: 1.9 us -> none  [shards(): sine = jnp.concatenate([-sine, sine], axis=1)]
    unnamed x12 -> x1, local copies, waits for them, and re-layouts: 3.26 us -> 1.88 us
where the time goes in v2:
time: 95.1 us; the launch traced here: 94.9 us
  Pallas kernels  93.1 us (98%)
  local copies, waits for them, and re-layouts  1.88 us (2%)
    pallas_call x1, Pallas kernels, shards(): pl.pallas_call(kernel, out_shape=jax.ShapeDtypeStruct((128, QH * HD), jnp...  93.1 us

profile of v2, /device:TPU:1, one launch (start us, length us, event | category | flops | bytes accessed | tf_op | source)
XLA Modules:
  0.0 94.9 jit_solution(7040218132059108105)
XLA Ops:
  0.0 93.1 %shard_map.55 = bf16[128,2048]{1,0:T(8,128)(2,1)} custom-call(s32[1,32]{1,0:T(1,128)} %order_hbm.1, s32[1,64]{1,0:T(1,128)} %bitcast.7, bf16[128,4096]{1,0:T(8,128)(2,1)} %bitcast.5, bf16[128,2048]{1,0:T(8,128)(2,1)} %bitcast.6, bf16[128,2048]{1,0:T(8,128)(2,1)} %pw.1), custom_call_target="tpu_custom_call" | custom-call | tf_op jit(solution)/shard_map/pallas_call | solution.py:435
  93.1 1.9 %copy.7 = bf16[1,128,2048]{2,1,0:T(8,128)(2,1)} copy(bf16[1,128,2048]{2,1,0:T(8,128)(2,1)} %bitcast.4) | data formatting | bytes 1048576

commit v3 on v2

--- a/solution.py
+++ b/solution.py
@@ -31,7 +31,7 @@
 def kernel(
     order_hbm, divisor_hbm, hid, qry, pw, out,
     order_ref, divisor_ref, cos_ref, sin_ref, wbuf, hbuf, qbuf, qrot, kvbuf, m_ref, l_ref, acc_ref, obuf,
-    ssem, rsem, lsem,
+    sa_ref, sb_ref, ta_ref, tb_ref, ssem, rsem, lsem,
 ):
     dp = lax.axis_index("dp")
     u = lax.axis_index("ulysses")
@@ -183,6 +183,16 @@
                         arrive(kbundle(g, zz), WAZ[way] + 2 * (h - 1) + g)
                     if h < last:
                         send(kbundle(g, zz), kbundle(g, zz), WAZ[way] + 2 * h + g, zdev(-step))
+
+    def side(a):
+        arrive(hbuf.at[x_minus, a, core], HX + a)
+        if a == 1:
+            send(hbuf.at[x_minus, 1, core], hbuf.at[x_minus, 1, core], HR + 1, chip(1, core))
+        send(hbuf.at[x_minus, a, core], hbuf.at[x_minus, a, core], HP + 2 + a, ul(partner))
+        arrive(hbuf.at[x_plus, a, core], HX + 2 + a)
+        if a == 0:
+            send(hbuf.at[x_plus, 0, core], hbuf.at[x_plus, 0, core], HR, chip(3, core))
+        send(hbuf.at[x_plus, a, core], hbuf.at[x_plus, a, core], HP + 4 + a, ul(partner))
 
     v_spread(0, own_v)
     v_hop(1)
@@ -226,6 +236,7 @@
 
     v_across(-3, 3)
     k_hop(3)
+    side(0)
     v_across(-4)
     k_hop(4)
     for offset in spots:
@@ -261,32 +272,10 @@
             landed(d - 1, n)
         send(kv_region(d - 1, n), kv_region(d, n), KV + (d - 1) * 8 + n, next_blk)
 
-    def side(a):
-        arrive(hbuf.at[x_minus, a, core], HX + a)
-        if a == 1:
-            send(hbuf.at[x_minus, 1, core], hbuf.at[x_minus, 1, core], HR + 1, chip(1, core))
-        send(hbuf.at[x_minus, a, core], hbuf.at[x_minus, a, core], HP + 2 + a, ul(partner))
-        arrive(hbuf.at[x_plus, a, core], HX + 2 + a)
-        if a == 0:
-            send(hbuf.at[x_plus, 0, core], hbuf.at[x_plus, 0, core], HR, chip(3, core))
-        send(hbuf.at[x_plus, a, core], hbuf.at[x_plus, a, core], HP + 4 + a, ul(partner))
-
     def side_partner(a):
         arrive(hbuf.at[x_minus, a, other_core], HP + 2 + a)
         arrive(hbuf.at[x_plus, a, other_core], HP + 4 + a)
 
-    for a in range(2):
-        local[2 + a].wait()
-        arrive(hbuf.at[x, a, other_core], HP + a)
-        project(a)
-    side(0)
-    side_partner(0)
-    project(2)
-    project(3)
-
-    local[4].wait()
-    for o in range(1, UL):
-        arrive(qbuf.at[lax.rem(u + UL - o, UL)], QX + o - 1)
 
     def rope_slice(s, carry):
         at = pl.ds(pl.multiple_of(s * 128, 128), 128)
@@ -299,106 +288,138 @@
             qrot[place, pl.ds(pl.multiple_of(lax.rem(s, 2) * 128, 128), 128)] = q.astype(jnp.bfloat16)
         return carry
 
-    lax.fori_loop(0, UL, rope_slice, 0)
+    def queries():
+        local[4].wait()
+        for o in range(1, UL):
+            arrive(qbuf.at[lax.rem(u + UL - o, UL)], QX + o - 1)
+        lax.fori_loop(0, UL, rope_slice, 0)
+
+    def far(a):
+        arrive(hbuf.at[x_far, a, core], HR + a)
+        send(hbuf.at[x_far, a, core], hbuf.at[x_far, a, core], HP + 6 + a, ul(partner))
 
     def attend(first, count, *tiles):
+        def shut(j, d, c):
+            source = lax.rem(blk + 16 - d, 16)
+            return order_ref[0, 2 * source + chunk[c] // 2] > order_ref[0, 2 * blk + j // 2]
+
+        def measure(s_ref, top_ref, j, head):
+            query = qrot[2 * j + head]
+            top = None
+            for t, (d, c) in enumerate(tiles):
+                keys = kvbuf[d, chunk[c], :, 0].reshape(256, HD)
+                score = lax.dot_general(
+                    keys, query, (((1,), (1,)), ((), ())), preferred_element_type=jnp.float32
+                )
+                if d == 0:
+                    row = lax.broadcasted_iota(jnp.int32, score.shape, 0)
+                    shift = (lax.shift_right_logical(row, 6) & 1) - lax.shift_right_logical(row, 7)
+                    key_at = row + 64 * shift + lax.rem(chunk[c], 2) * 256
+                    apart = lax.rem(chunk[c] // 2 + j // 2, 2)
+                    query_at = lax.broadcasted_iota(jnp.int32, score.shape, 1) + (
+                        lax.rem(j, 2) * 256 + apart * 1024
+                    )
+                    score = jnp.where(query_at >= key_at, score, 4.0 * NEG)
+                s_ref[t] = score
+                here = jnp.max(score, axis=0, keepdims=True) + jnp.where(shut(j, d, c), -FAR, 0.0)
+                top = here if top is None else jnp.maximum(top, here)
+            top_ref[...] = top
+
+        def gather(s_ref, top_ref, j, head):
+            place = 2 * j + head
+            old = m_ref[place]
+            new = jnp.maximum(old, top_ref[...])
+            shrink = jnp.exp2((old - new) * SCALE2)
+            total = l_ref[place] * shrink
+            mixed = acc_ref[place] * shrink
+            for t, (d, c) in enumerate(tiles):
+                base = new + jnp.where(shut(j, d, c), FAR, 0.0)
+                weight = jnp.exp2((s_ref[t] - base) * SCALE2)
+                total = total + jnp.sum(weight.reshape(32, 8, 256), axis=0)
+                values = jnp.concatenate([kvbuf[d, chunk[c], 0, 1], kvbuf[d, chunk[c], 1, 1]], axis=1)
+                mixed = mixed + jnp.dot(
+                    values, weight.astype(jnp.bfloat16), preferred_element_type=jnp.float32
+                )
+            l_ref[place] = total
+            acc_ref[place] = mixed
+            m_ref[place] = new
+
+        measure(sa_ref, ta_ref, first, 0)
+        if count == 1:
+            measure(sb_ref, tb_ref, first, 1)
+            gather(sa_ref, ta_ref, first, 0)
+            gather(sb_ref, tb_ref, first, 1)
+            return
+
         def one_chip(i, carry):
             j = first + i
-            query_order = order_ref[0, 2 * blk + j // 2]
-            lows, lifts = [], []
-            for d, c in tiles:
-                source = lax.rem(blk + 16 - d, 16)
-                shut = order_ref[0, 2 * source + chunk[c] // 2] > query_order
-                lows.append(jnp.where(shut, -FAR, 0.0))
-                lifts.append(jnp.where(shut, FAR, 0.0))
-            for head in range(2):
-                place = 2 * j + head
-                query = qrot[place]
-                old = m_ref[place]
-                new = old
-                scores = []
-                for (d, c), low in zip(tiles, lows):
-                    keys = kvbuf[d, chunk[c], :, 0].reshape(256, HD)
-                    score = lax.dot_general(
-                        keys, query, (((1,), (1,)), ((), ())), preferred_element_type=jnp.float32
-                    )
-                    if d == 0:
-                        row = lax.broadcasted_iota(jnp.int32, score.shape, 0)
-                        shift = (lax.shift_right_logical(row, 6) & 1) - lax.shift_right_logical(row, 7)
-                        key_at = row + 64 * shift + lax.rem(chunk[c], 2) * 256
-                        apart = lax.rem(chunk[c] // 2 + j // 2, 2)
-                        query_at = lax.broadcasted_iota(jnp.int32, score.shape, 1) + (
-                            lax.rem(j, 2) * 256 + apart * 1024
-                        )
-                        score = jnp.where(query_at >= key_at, score, 4.0 * NEG)
-                    scores.append(score)
-                    new = jnp.maximum(new, jnp.max(score, axis=0, keepdims=True) + low)
-                shrink = jnp.exp2((old - new) * SCALE2)
-                total = l_ref[place] * shrink
-                mixed = acc_ref[place] * shrink
-                for (d, c), score, lift in zip(tiles, scores, lifts):
-                    weight = jnp.exp2((score - (new + lift)) * SCALE2)
-                    total = total + jnp.sum(weight.reshape(32, 8, 256), axis=0)
-                    values = jnp.concatenate([kvbuf[d, chunk[c], 0, 1], kvbuf[d, chunk[c], 1, 1]], axis=1)
-                    mixed = mixed + jnp.dot(
-                        values, weight.astype(jnp.bfloat16), preferred_element_type=jnp.float32
-                    )
-                l_ref[place] = total
-                acc_ref[place] = mixed
-                m_ref[place] = new
+            measure(sb_ref, tb_ref, j, 1)
+            gather(sa_ref, ta_ref, j, 0)
+            measure(sa_ref, ta_ref, first + jnp.minimum(i + 1, count - 1), 0)
+            gather(sb_ref, tb_ref, j, 1)
             return carry
 
         lax.fori_loop(0, count, one_chip, 0)
 
+    local[2].wait()
+    arrive(hbuf.at[x, 0, other_core], HP + 0)
+    project(0)
+    local[3].wait()
+    arrive(hbuf.at[x, 1, other_core], HP + 1)
+    project(1)
+    queries()
+    side_partner(0)
+    project(2)
     pass_on(2, 0)
+    project(3)
     pass_on(2, 1)
+    attend(0, 2, (0, 0), (1, 0))
+    attend(2, 2, (0, 0), (1, 0))
     pass_on(2, 2)
+    pass_on(3, 0)
+    side(1)
     pass_on(2, 3)
-    attend(0, 2, (0, 0), (1, 0))
-    pass_on(3, 0)
-    pass_on(3, 1)
-    attend(2, 2, (0, 0), (1, 0))
-    side(1)
     side_partner(1)
     project(4)
+    pass_on(3, 1)
     project(5)
+    attend(0, 2, (0, 1), (0, 2))
     pass_on(3, 2)
+    attend(2, 2, (0, 1), (0, 2))
     pass_on(3, 3)
-    attend(0, 4, (0, 1), (0, 2))
     pass_on(2, 4)
+    attend(0, 2, (1, 1), (2, 0))
+    attend(2, 2, (1, 1), (2, 0))
     pass_on(2, 5)
     landed(3, 0)
     landed(3, 1)
-    attend(0, 2, (2, 0), (3, 0))
+    attend(0, 2, (1, 2), (3, 0))
+    attend(2, 2, (1, 2), (3, 0))
+    far(0)
+    far(1)
     pass_on(3, 4)
-    pass_on(3, 5)
-    attend(2, 2, (2, 0), (3, 0))
-    arrive(hbuf.at[x_far, 0, core], HR)
-    send(hbuf.at[x_far, 0, core], hbuf.at[x_far, 0, core], HP + 6, ul(partner))
-    attend(0, 2, (1, 1), (1, 2))
     arrive(hbuf.at[x_far, 0, other_core], HP + 6)
     project(6)
-    arrive(hbuf.at[x_far, 1, core], HR + 1)
-    send(hbuf.at[x_far, 1, core], hbuf.at[x_far, 1, core], HP + 7, ul(partner))
-    attend(2, 2, (1, 1), (1, 2))
     arrive(hbuf.at[x_far, 1, other_core], HP + 7)
     project(7)
+    pass_on(3, 5)
+    attend(0, 2, (0, 3), (2, 1))
+    attend(2, 2, (0, 3), (2, 1))
+    landed(3, 2)
+    landed(3, 4)
+    attend(0, 2, (2, 2), (3, 1))
     pass_on(2, 6)
-    attend(0, 2, (2, 1), (2, 2))
+    attend(2, 2, (2, 2), (3, 1))
     pass_on(2, 7)
-    attend(2, 2, (2, 1), (2, 2))
+    landed(3, 3)
+    landed(3, 5)
+    attend(0, 2, (1, 3), (3, 2))
+    attend(2, 2, (1, 3), (3, 2))
     pass_on(3, 6)
-    for n in (2, 4):
-        landed(3, n)
-    attend(0, 2, (0, 3), (3, 1))
     pass_on(3, 7)
-    attend(2, 2, (0, 3), (3, 1))
-    for n in (3, 5):
-        landed(3, n)
-    attend(0, 4, (3, 2), (1, 3))
     attend(0, 4, (2, 3))
-    for n in (6, 7):
-        landed(3, n)
+    landed(3, 6)
+    landed(3, 7)
 
     here = out.at[:, pl.ds(pl.multiple_of(u * 2 * HD, HD), 2 * HD)]
     own_out = pltpu.make_async_copy(obuf.at[u], here, lsem.at[5])
@@ -453,6 +474,10 @@
             pltpu.VMEM((8, 8, 256), jnp.float32),
             pltpu.VMEM((8, HD, 256), jnp.float32),
             pltpu.VMEM((UL, 128, 2 * HD), jnp.bfloat16),
+            pltpu.VMEM((2, 256, 256), jnp.float32),
+            pltpu.VMEM((2, 256, 256), jnp.float32),
+            pltpu.VMEM((1, 256), jnp.float32),
+            pltpu.VMEM((1, 256), jnp.float32),
             pltpu.SemaphoreType.DMA((104,)),
             pltpu.SemaphoreType.DMA((104,)),
             pltpu.SemaphoreType.DMA((8,)),

time: 95.1 us -> 83 us (0.87)
  Pallas kernels: 93.1 us -> 81 us
    pallas_call x1, Pallas kernels: 93.1 us -> 81 us  [shards(): pl.pallas_call(kernel, out_shape=jax.ShapeDtypeStruct((128, QH * HD), jnp...]
where the time goes in v3:
time: 83 us; the launch traced here: 82.9 us
  Pallas kernels  81 us (98%)
  local copies, waits for them, and re-layouts  1.88 us (2%)
    pallas_call x1, Pallas kernels, shards(): pl.pallas_call(kernel, out_shape=jax.ShapeDtypeStruct((128, QH * HD), jnp...  81 us
    unnamed x1, local copies, waits for them, and re-layouts  1.88 us

profile of v3, /device:TPU:1, one launch (start us, length us, event | category | flops | bytes accessed | tf_op | source)
XLA Modules:
  0.0 82.9 jit_solution(3818480466668332947)
XLA Ops:
  0.0 81.0 %shard_map.55 = bf16[128,2048]{1,0:T(8,128)(2,1)} custom-call(s32[1,32]{1,0:T(1,128)} %order_hbm.1, s32[1,64]{1,0:T(1,128)} %bitcast.7, bf16[128,4096]{1,0:T(8,128)(2,1)} %bitcast.5, bf16[128,2048]{1,0:T(8,128)(2,1)} %bitcast.6, bf16[128,2048]{1,0:T(8,128)(2,1)} %pw.1), custom_call_target="tpu_custom_call" | custom-call | tf_op jit(solution)/shard_map/pallas_call | solution.py:456
  81.0 1.9 %copy.7 = bf16[1,128,2048]{2,1,0:T(8,128)(2,1)} copy(bf16[1,128,2048]{2,1,0:T(8,128)(2,1)} %bitcast.4) | data formatting | bytes 1048576

commit v4 on v3

--- a/solution.py
+++ b/solution.py
@@ -30,7 +30,7 @@
 
 def kernel(
     order_hbm, divisor_hbm, hid, qry, pw, out,
-    order_ref, divisor_ref, cos_ref, sin_ref, wbuf, hbuf, qbuf, qrot, kvbuf, m_ref, l_ref, acc_ref, obuf,
+    order_ref, divisor_ref, cos_ref, sin_ref, wk_ref, wv_ref, hbuf, qbuf, qrot, kvbuf, m_ref, l_ref, acc_ref, obuf,
     sa_ref, sb_ref, ta_ref, tb_ref, ssem, rsem, lsem,
 ):
     dp = lax.axis_index("dp")
@@ -88,7 +88,7 @@
     own_v = pw.at[:, pl.ds(pl.multiple_of(KVH * HD + u * HD, HD), HD)]
     WB = (take(4), take(3))
     WAY = take(3)
-    WAZ = (take(8), take(8))
+    WAZ = (take(16), take(16))
     WBY = (take(8), take(8))
     WBF = take(8)
     HX, HR, HP = take(4), take(2), take(8)
@@ -97,13 +97,10 @@
     OX = take(7)
 
     def vpiece(yy, zz):
-        return wbuf.at[lax.rem(yy, 2), yy // 2, zz, :, pl.ds(HD, HD)]
+        return wv_ref.at[lax.rem(yy, 2), yy // 2, zz]
 
     def kpiece(yy, zz):
-        return wbuf.at[lax.rem(yy, 2), yy // 2, zz, :, pl.ds(0, HD)]
-
-    def kbundle(g, zz):
-        return wbuf.at[g, :, zz, :, pl.ds(0, HD)]
+        return wk_ref.at[lax.rem(yy, 2), yy // 2, zz]
 
     def hid_half(a):
         return hid.at[pl.ds(a * 64, 64)]
@@ -126,15 +123,17 @@
     barrier = pltpu.get_barrier_semaphore()
     greet = [ul(lax.rem(u + o, UL)) for o in range(1, UL)]
     greet += [ydev(o) for o in range(1, 4)]
-    greet += [zdev(1), zdev(-1), next_blk, prev_blk]
+    greet += [zdev(1), zdev(-1), zdev(2), zdev(-2), next_blk, prev_blk]
     for device in greet:
         pl.semaphore_signal(barrier, inc=1, device_id=device, device_id_type=MESH)
     pl.semaphore_wait(barrier, len(greet))
 
     send(own_v, vpiece(y, z), WB[0], zdev(1))
     send(own_v, vpiece(y, z), WB[1], zdev(-1))
-    for o in (2, 1, 3):
-        send(own_k, kpiece(y, z), WAY + o - 1, ydev(o))
+    send(own_v, vpiece(y, z), WB[0] + 1, zdev(2))
+    send(own_v, vpiece(y, z), WB[1] + 1, zdev(-2))
+    for o, spot in ((2, 2), (1, 0), (3, 1)):
+        send(own_k, kpiece(y, z), WAY + spot, ydev(o))
     for a in range(2):
         send(hid_half(a), hbuf.at[x, a, core], HX + a, chip(1, core))
         send(hid_half(a), hbuf.at[x, a, core], HX + 2 + a, chip(3, core))
@@ -156,10 +155,12 @@
     def v_hop(h):
         for way, step in ((0, -1), (1, 1)):
             if h <= (4, 3)[way]:
-                zz = wrap(z + step * h, NZ)
-                arrive(vpiece(y, zz), WB[way] + h - 1)
-                if h < (4, 3)[way]:
-                    send(vpiece(y, zz), vpiece(y, zz), WB[way] + h, zdev(-step))
+                piece = vpiece(y, wrap(z + step * h, NZ))
+                arrive(piece, WB[way] + h - 1)
+                if h == 2:
+                    send(piece, piece, WB[way] + 2, zdev(-step))
+                    if way == 0:
+                        send(piece, piece, WB[way] + 3, zdev(2))
                 v_spread(step * h)
 
     def v_across(*offsets):
@@ -173,16 +174,24 @@
             if spot % 2 == 1:
                 send(vpiece(y_up, zz), vpiece(y_up, zz), WBF + spot, ydev(3))
 
-    def k_hop(h):
-        for g in range(2):
+    k_from = (y, y_down, y_up, y_far)
+    k_last = ((4, 3), (4, 3), (3, 4), (3, 4))
+
+    def k_start(p):
+        if p:
+            arrive(kpiece(k_from[p], z), WAY + p - 1)
+        src = kpiece(k_from[p], z) if p else own_k
+        for way, step in ((0, -1), (1, 1)):
+            send(src, kpiece(k_from[p], z), WAZ[way] + 4 * p, zdev(-step))
+
+    def k_hop(h, *which):
+        for p in which:
             for way, step in ((0, -1), (1, 1)):
-                last = 4 if g == way else 3
-                if h <= last:
-                    zz = wrap(z + step * h, NZ)
-                    if h > 0:
-                        arrive(kbundle(g, zz), WAZ[way] + 2 * (h - 1) + g)
-                    if h < last:
-                        send(kbundle(g, zz), kbundle(g, zz), WAZ[way] + 2 * h + g, zdev(-step))
+                if h <= k_last[p][way]:
+                    piece = kpiece(k_from[p], wrap(z + step * h, NZ))
+                    arrive(piece, WAZ[way] + 4 * p + h - 1)
+                    if h < k_last[p][way]:
+                        send(piece, piece, WAZ[way] + 4 * p + h, zdev(-step))
 
     def side(a):
         arrive(hbuf.at[x_minus, a, core], HX + a)
@@ -194,20 +203,28 @@
             send(hbuf.at[x_plus, 0, core], hbuf.at[x_plus, 0, core], HR, chip(3, core))
         send(hbuf.at[x_plus, a, core], hbuf.at[x_plus, a, core], HP + 4 + a, ul(partner))
 
+    k_start(0)
     v_spread(0, own_v)
     v_hop(1)
-    local[0].wait()
-    for o in range(1, 4):
-        arrive(kpiece(lax.rem(y + 4 - o, 4), z), WAY + o - 1)
-    k_hop(0)
+    k_start(1)
+    k_start(2)
     v_hop(2)
     v_across(0)
+    k_start(3)
+    k_hop(1, 0)
+    v_across(-1, 1)
+    k_hop(1, 1, 2)
     v_hop(3)
-    v_across(-1, 1)
-    k_hop(1)
     v_hop(4)
+    k_hop(1, 3)
     v_across(-2, 2)
-    k_hop(2)
+    k_hop(2, 0, 1, 2)
+    v_across(-3, 3)
+    k_hop(2, 3)
+    k_hop(3, 0)
+    v_across(-4)
+    k_hop(3, 1, 2, 3)
+    side(0)
 
     local[5].wait()
     local[6].wait()
@@ -234,11 +251,8 @@
     l_ref[...] = jnp.zeros_like(l_ref)
     acc_ref[...] = jnp.zeros_like(acc_ref)
 
-    v_across(-3, 3)
-    k_hop(3)
-    side(0)
-    v_across(-4)
-    k_hop(4)
+    local[0].wait()
+    k_hop(4, 0, 1, 2, 3)
     for offset in spots:
         arrive(vpiece(y_far, wrap(z + offset, NZ)), WBF + spots[offset])
     local[1].wait()
@@ -249,7 +263,7 @@
     def project(n):
         xc, a = chunk[pieces[n][0]], pieces[n][1]
         rows = hbuf[xc, a].reshape(128, 4096)
-        weight = wbuf[...].reshape(4096, 2 * HD)
+        weight = jnp.concatenate([wk_ref[...].reshape(4096, HD), wv_ref[...].reshape(4096, HD)], axis=1)
         result = jnp.dot(rows, weight, preferred_element_type=jnp.float32)
         key = result[:, :HD]
         turned = pltpu.roll(key, HD // 2, 1)
@@ -370,22 +384,22 @@
     queries()
     side_partner(0)
     project(2)
+    project(3)
     pass_on(2, 0)
-    project(3)
     pass_on(2, 1)
     attend(0, 2, (0, 0), (1, 0))
     attend(2, 2, (0, 0), (1, 0))
     pass_on(2, 2)
+    pass_on(2, 3)
+    side(1)
     pass_on(3, 0)
-    side(1)
-    pass_on(2, 3)
     side_partner(1)
     project(4)
+    project(5)
     pass_on(3, 1)
-    project(5)
     attend(0, 2, (0, 1), (0, 2))
+    attend(2, 2, (0, 1), (0, 2))
     pass_on(3, 2)
-    attend(2, 2, (0, 1), (0, 2))
     pass_on(3, 3)
     pass_on(2, 4)
     attend(0, 2, (1, 1), (2, 0))
@@ -397,18 +411,18 @@
     attend(2, 2, (1, 2), (3, 0))
     far(0)
     far(1)
-    pass_on(3, 4)
     arrive(hbuf.at[x_far, 0, other_core], HP + 6)
     project(6)
+    pass_on(3, 4)
     arrive(hbuf.at[x_far, 1, other_core], HP + 7)
     project(7)
+    attend(0, 2, (0, 3), (2, 1))
     pass_on(3, 5)
-    attend(0, 2, (0, 3), (2, 1))
     attend(2, 2, (0, 3), (2, 1))
+    pass_on(2, 6)
     landed(3, 2)
     landed(3, 4)
     attend(0, 2, (2, 2), (3, 1))
-    pass_on(2, 6)
     attend(2, 2, (2, 2), (3, 1))
     pass_on(2, 7)
     landed(3, 3)
@@ -465,7 +479,8 @@
             pltpu.VMEM((1, HD // 2), jnp.int32),
             pltpu.VMEM((1024, HD), jnp.float32),
             pltpu.VMEM((1024, HD), jnp.float32),
-            pltpu.VMEM((2, 2, NZ, 128, 2 * HD), jnp.bfloat16),
+            pltpu.VMEM((2, 2, NZ, 128, HD), jnp.bfloat16),
+            pltpu.VMEM((2, 2, NZ, 128, HD), jnp.bfloat16),
             pltpu.VMEM((4, 2, 2, 64, 4096), jnp.bfloat16),
             pltpu.VMEM((UL, 128, 2 * HD), jnp.bfloat16),
             pltpu.VMEM((8, 256, HD), jnp.bfloat16),
@@ -478,8 +493,8 @@
             pltpu.VMEM((2, 256, 256), jnp.float32),
             pltpu.VMEM((1, 256), jnp.float32),
             pltpu.VMEM((1, 256), jnp.float32),
-            pltpu.SemaphoreType.DMA((104,)),
-            pltpu.SemaphoreType.DMA((104,)),
+            pltpu.SemaphoreType.DMA((120,)),
+            pltpu.SemaphoreType.DMA((120,)),
             pltpu.SemaphoreType.DMA((8,)),
         ],
         compiler_params=pltpu.CompilerParams(

time: 83 us -> 81.6 us (0.983)
  Pallas kernels: 81 us -> 79.6 us
    pallas_call x1, Pallas kernels: 81 us -> 79.6 us  [shards(): pl.pallas_call(kernel, out_shape=jax.ShapeDtypeStruct((128, QH * HD), jnp...]
where the time goes in v4:
time: 81.6 us; the launch traced here: 81.5 us
  Pallas kernels  79.6 us (98%)
  local copies, waits for them, and re-layouts  1.88 us (2%)
    pallas_call x1, Pallas kernels, shards(): pl.pallas_call(kernel, out_shape=jax.ShapeDtypeStruct((128, QH * HD), jnp...  79.6 us
    unnamed x1, local copies, waits for them, and re-layouts  1.88 us

profile of v4, /device:TPU:1, one launch (start us, length us, event | category | flops | bytes accessed | tf_op | source)
XLA Modules:
  0.0 81.5 jit_solution(9208694005360565711)
XLA Ops:
  0.0 79.6 %shard_map.55 = bf16[128,2048]{1,0:T(8,128)(2,1)} custom-call(s32[1,32]{1,0:T(1,128)} %order_hbm.1, s32[1,64]{1,0:T(1,128)} %bitcast.7, bf16[128,4096]{1,0:T(8,128)(2,1)} %bitcast.5, bf16[128,2048]{1,0:T(8,128)(2,1)} %bitcast.6, bf16[128,2048]{1,0:T(8,128)(2,1)} %pw.1), custom_call_target="tpu_custom_call" | custom-call | tf_op jit(solution)/shard_map/pallas_call | solution.py:470
  79.6 1.9 %copy.7 = bf16[1,128,2048]{2,1,0:T(8,128)(2,1)} copy(bf16[1,128,2048]{2,1,0:T(8,128)(2,1)} %bitcast.4) | data formatting | bytes 1048576
